TPU v7x, 32 devices: a whole 2x2x4 slice. The times are simulated.
32 devices in a mesh: wide: 8 (over y, x, core), narrow: 4 (over z).
Axes of the slice: x: 2, y: 2, z: 4, core: 2. Of those that a mesh axis runs over, the one named last changes fastest.
Arguments:
- loads: bfloat16 [256, 262144], P('narrow', 'wide'), may hold values from -6 to 6
- state: bfloat16 [256, 262144], P('narrow', 'wide'), may hold values from -6 to 6
- modal_diag: float32 [262144], P('wide'), may hold values from 0.5 to 2
- phi: bfloat16 [2048, 128, 128], P('wide'), may hold values from -0.25 to 0.25
- incidence: int32 [2048], P('wide'), may hold values from 0 to 127
- sizes: int32 [1024], P('wide'), may hold values from 1 to 129, as said below
- factor: float32 [16384, 16384], P('wide', 'narrow'), may hold values from -0.046875 to 0.046875
Outputs:
- adjoint: bfloat16 [256, 262144], P('narrow', 'wide')
- sensitivity: float32 [256, 1024], P('narrow', 'wide')
Inputs may be any that keep to these rules, and one draw needn't show every extreme that they name: `sizes`: the 128 substructures of each group hold at most 256 tiles together, and in every draw some group holds exactly 256.
All inputs are finite; a program needn't handle non-finite values.
Results may differ from a plain program's by a relative error of at most 0.015.
Values may be sent and summed in bfloat16 or wider, within the bound.
A program may use at most 128 MiB of HBM per device.

v0:
```python
import jax
import jax.numpy as jnp
from jax import lax
from jax.sharding import PartitionSpec as P

sens_scale = 0.0625


def body(loads, state, modal_diag, phi, incidence, sizes, factor):
    load_cols = loads.shape[0]
    tile_count = phi.shape[0]
    block_rows = phi.shape[1]
    subs_local = sizes.shape[0]
    own_rows = factor.shape[0]
    modes_all = own_rows * lax.axis_size("wide")
    block_count = modes_all // block_rows
    load_tiles = loads.reshape(load_cols, tile_count, block_rows)
    state_tiles = state.reshape(load_cols, tile_count, block_rows)
    diag_tiles = modal_diag.reshape(tile_count, block_rows)
    slot_index = jnp.arange(tile_count, dtype=jnp.int32)
    running = jnp.cumsum(sizes)
    owner_sub = jnp.sum((running[None, :] <= slot_index[:, None]).astype(jnp.int32), axis=1)
    live_slot = slot_index < running[-1]
    member = (
        (owner_sub[:, None] == jnp.arange(subs_local, dtype=jnp.int32)[None, :])
        & live_slot[:, None]
    ).astype(jnp.float32)
    chooser = (
        (incidence[:, None] == jnp.arange(block_count, dtype=jnp.int32)[None, :])
        & live_slot[:, None]
    ).astype(jnp.float32)
    tile_terms = jnp.einsum("lti,tim->ltm", load_tiles, phi, preferred_element_type=jnp.float32)
    partial_value = jnp.einsum("tn,ltm->lnm", chooser, tile_terms, precision=lax.Precision.HIGHEST)
    partial_value = partial_value.reshape(load_cols, modes_all)
    own_loads = lax.psum_scatter(partial_value, "wide", scatter_dimension=1, tiled=True)
    image = jnp.dot(
        lax.all_gather(own_loads, "narrow", axis=0, tiled=True),
        factor,
        precision=lax.Precision.HIGHEST,
    )
    image = lax.psum(image.astype(jnp.bfloat16), "wide").astype(jnp.float32)
    own_amplitude = lax.psum_scatter(
        lax.dot_general(
            image, factor, (((1,), (1,)), ((), ())), precision=lax.Precision.HIGHEST
        ).astype(jnp.bfloat16),
        "narrow",
        scatter_dimension=0,
        tiled=True,
    )
    amp_all = lax.all_gather(own_amplitude, "wide", axis=1, tiled=True)
    picked = jnp.take(amp_all.reshape(load_cols, block_count, block_rows), incidence, axis=1)
    coupling = jnp.einsum("ltm,tim->lti", picked, phi, preferred_element_type=jnp.float32)
    response = diag_tiles[None, :, :] * load_tiles.astype(jnp.float32) + coupling
    response = jnp.where(live_slot[None, :, None], response, jnp.zeros_like(response))
    row_totals = jnp.sum(response * state_tiles.astype(jnp.float32), axis=2) * sens_scale
    sensitivity = jnp.dot(row_totals, member, precision=lax.Precision.HIGHEST)
    adjoint = response.astype(jnp.bfloat16).reshape(load_cols, tile_count * block_rows)
    return (adjoint, sensitivity)


def solution(mesh):
    return jax.shard_map(
        body,
        mesh=mesh,
        in_specs=(
            P("narrow", "wide"),
            P("narrow", "wide"),
            P("wide"),
            P("wide", None, None),
            P("wide"),
            P("wide"),
            P("wide", "narrow"),
        ),
        out_specs=(P("narrow", "wide"), P("narrow", "wide")),
        check_vma=False,
    )
```

profile of v0, /device:TPU:0, one launch (start us, length us, event | category | flops | bytes accessed | tf_op | source)
XLA Modules:
  0.0 344.6 jit_solution(5754433226566873415)
XLA Ops:
  7.2 0.8 copy.24
  8.0 0.2 reduce-window.4
  8.1 0.5 slice.7
  8.7 0.6 iota_compare_fusion.3
  9.3 7.0 %fusion.12 = f32[64,256,128]{2,0,1:T(8,128)S(1)} fusion(bf16[256,128,128]{2,1,0:T(8,128)(2,1)} %param.10, bf16[64,32768]{1,0:T(8,128)(2,1)} %param.7), kind=kOutput, calls=%fused_computation.19 | convolution fusion | flops 536870912 | bytes 20971520 | tf_op jit(solution)/shard_map/lti,tim->ltm/dot_general | solution.py:32
  16.3 15.3 %fusion.16 = f32[64,128,128]{1,2,0:T(8,128)} fusion(f32[64,256,128]{2,0,1:T(8,128)S(1)} %fusion.12, s32[256]{0:T(256)S(1)} %copy-done, pred[256]{0:T(512)(128)(4,1)S(1)} %iota_compare_fusion.3), kind=kOutput, calls=%fused_computation.22 | convolution fusion | flops 3221291008 | bytes 12584192 | tf_op jit(solution)/shard_map/tn,ltm->lnm/dot_general | solution.py:33
  31.6 5.6 %copy.28 = f32[64,128,128]{2,1,0:T(8,128)} copy(f32[64,128,128]{1,2,0:T(8,128)} %fusion.16) | data formatting | bytes 8388608 | tf_op jit(solution)/shard_map/tn,ltm->lnm/transpose | solution.py:33
  37.2 6.6 %copy.51 = f32[8,8,128,128]{3,1,2,0:T(8,128)} copy(f32[8,8,128,128]{3,2,1,0:T(8,128)} %bitcast.66) | data formatting | bytes 8388608
  43.8 53.9 %reduce-scatter.3.cloned.1.call-done = f32[64,2048]{1,0:T(8,128)} async-done(((f32[64,16384]{1,0:T(8,128)}), f32[64,2048]{1,0:T(8,128)}) %reduce-scatter.3.cloned.1.call-update) | async-done | bytes 524304 | tf_op jit(solution)/shard_map/reduce_scatter | solution.py:35
  97.8 47.2 %all-gather.3.cloned.1.call-done = f32[256,2048]{1,0:T(8,128)} async-done(((f32[64,2048]{1,0:T(8,128)}), f32[256,2048]{1,0:T(8,128)}) %all-gather.3.cloned.1.call-update) | async-done | bytes 2097168 | tf_op jit(solution)/shard_map/all_gather | solution.py:37
  145.0 33.8 %convolution_convert_fusion = bf16[256,4096]{1,0:T(8,128)(2,1)} fusion(f32[256,2048]{1,0:T(8,128)} %all-gather.3.cloned.1.call-done, f32[2048,4096]{1,0:T(8,128)} %param.13), kind=kOutput, calls=%fused_computation.8 | convolution fusion | flops 25770852352 | bytes 37748736 | tf_op jit(solution)/shard_map/dot_general | solution.py:36
  178.8 0.0 reduce-scatter.5.cloned.1.call-start
  178.9 60.7 %all-reduce.2.cloned.1.call-done = bf16[256,4096]{1,0:T(8,128)(2,1)} async-done(((bf16[256,4096]{1,0:T(8,128)(2,1)}), bf16[256,4096]{1,0:T(8,128)(2,1)}) %all-reduce.2.cloned.1.call-update) | async-done | bytes 2097168 | tf_op jit(solution)/shard_map/psum | solution.py:41
  239.6 23.8 %convolution_convert_fusion.1 = bf16[256,2048]{1,0:T(8,128)(2,1)} fusion(bf16[256,4096]{1,0:T(8,128)(2,1)} %all-reduce.2.cloned.1.call-done, f32[2048,4096]{1,0:T(8,128)} %param.13), kind=kOutput, calls=%fused_computation.21 | convolution fusion | flops 25770328064 | bytes 36700160 | tf_op jit(solution)/shard_map/dot_general | solution.py:43
  263.4 0.0 all-gather.5.cloned.1.call-start
  263.4 26.5 %reduce-scatter.5.cloned.1.call-done = bf16[64,2048]{1,0:T(8,128)(2,1)} async-done(((bf16[256,2048]{1,0:T(8,128)(2,1)}), bf16[64,2048]{1,0:T(8,128)(2,1)}) %reduce-scatter.5.cloned.1.call-update) | async-done | bytes 262160 | tf_op jit(solution)/shard_map/reduce_scatter | solution.py:42
  289.9 0.1 reduce
  290.1 0.1 convert_reduce_fusion
  290.2 27.8 %all-gather.5.cloned.1.call-done = bf16[64,16384]{1,0:T(8,128)(2,1)} async-done(((bf16[64,2048]{1,0:T(8,128)(2,1)}), bf16[64,16384]{1,0:T(8,128)(2,1)}) %all-gather.5.cloned.1.call-update) | async-done | bytes 2097168 | tf_op jit(solution)/shard_map/all_gather | solution.py:50
  318.0 2.2 copy_bitcast_fusion.2
  320.1 3.1 gather_fusion
  323.3 11.1 %fusion = (f32[64,256]{0,1:T(8,128)S(1)}, bf16[256,8,8,128]{3,2,1,0:T(8,128)(2,1)S(1)}) fusion(f32[256,128]{1,0:T(8,128)S(1)} %bitcast.69, pred[256]{0:T(512)(128)(4,1)S(1)} %iota_compare_fusion.3, bf16[256,128,128]{2,1,0:T(8,128)(2,1)} %param.10, bf16[256,64,128]{2,1,0:T(8,128)(2,1)} %gather_fusion, pred[256]{0:T(512)(128)(4,1)S(1)} %compare_and_fusion, ...), kind=kOutput, calls=%fused_computation.2 | convolution fusion | flops 555728896 | bytes 25362944 | tf_op jit(solution)/shard_map/ltm,tim->lti/dot_general | solution.py:52
  334.4 2.8 copy.52
  337.1 1.0 fusion.20
  (15 shorter events, 0.2 us)
Async XLA Ops:
  7.2 90.6 %reduce-scatter.3.cloned.1.call-start = ((), (), s32[]{:S(2)}) async-start(), calls=%async_computation.2 | async-start | bytes 4718592 | tf_op jit(solution)/shard_map/reduce_scatter | solution.py:35
  9.3 7.0 %copy-start = (s32[256]{0:T(256)S(1)}, s32[256]{0:T(256)}, u32[]{:S(2)}) copy-start(s32[256]{0:T(256)} %param.11) | copy-start | bytes 3076
  43.8 101.2 %all-gather.3.cloned.1.call-start = ((), (), s32[]{:S(2)}) async-start(), calls=%async_computation.3 | async-start | bytes 2621440 | tf_op jit(solution)/shard_map/all_gather | solution.py:37
  97.8 141.8 %all-reduce.2.cloned.1.call-start = ((), (), s32[]{:S(2)}) async-start(), calls=%async_computation.4 | async-start | bytes 4194304 | tf_op jit(solution)/shard_map/psum | solution.py:41
  178.8 111.1 %reduce-scatter.5.cloned.1.call-start = ((), (), s32[]{:S(2)}) async-start(), calls=%async_computation.5 | async-start | bytes 1310720 | tf_op jit(solution)/shard_map/reduce_scatter | solution.py:42
  263.4 54.6 %all-gather.5.cloned.1.call-start = ((), (), s32[]{:S(2)}) async-start(), calls=%async_computation.6 | async-start | bytes 2359296 | tf_op jit(solution)/shard_map/all_gather | solution.py:50
  320.1 3.1 copy-start.1
Sparse Core Ops, SparseCore 0:
  43.9 53.8 reduce-scatter.2
  99.3 45.6 all-gather.2
  179.0 60.5 all-reduce.1
  263.5 26.3 reduce-scatter.4
  291.6 26.2 all-gather.4
where the time goes:
time: 345 us
  waiting for transfers between devices  216 us (63%)
  matrix products  91.9 us (27%)
  local copies, waits for them, and re-layouts  21.5 us (6%)
  between operations  13.9 us (4%)
    psum x1, waiting for transfers between devices, body(): image = lax.psum(image.astype(jnp.bfloat16), 'wide').astype(jnp.float32)  60.7 us
    reduce_scatter x1, waiting for transfers between devices, body(): lax.psum_scatter(partial_value, 'wide', scatter_dimension=1, tiled=True)  53.9 us
    all_gather x1, waiting for transfers between devices, body(): lax.all_gather(own_loads, 'narrow', axis=0, tiled=True)  47.2 us
    dot_general x1, matrix products, body(): jnp.dot(lax.all_gather(own_loads, 'narrow', axis=0, tiled=True), factor,...  33.8 us
    all_gather x1, waiting for transfers between devices, body(): amp_all = lax.all_gather(own_amplitude, 'wide', axis=1, tiled=True)  27.8 us
    reduce_scatter x1, waiting for transfers between devices, body(): lax.psum_scatter(lax.dot_general(image, factor, (((1,), (1,)), ((), ())),...  26.5 us
    dot_general x1, matrix products, body(): lax.dot_general(image, factor, (((1,), (1,)), ((), ())), precision=lax.Pr...  23.8 us
    dot_general x1, matrix products, body(): jnp.einsum('tn,ltm->lnm', chooser, tile_terms, precision=lax.Precision.HI...  15.3 us
  transfers between devices with their start and end apart: 5, of which 5 were waited for; matrix products, arithmetic and copies ran while one was open for 0% of the time, Pallas kernels for 0%

commit v1 on v0

v1 whole, which is shorter than its diff:
```python
import functools
import itertools
import jax
import jax.numpy as jnp
from jax import lax
from jax.experimental import pallas as pl
from jax.experimental.pallas import tpu as pltpu
from jax.sharding import PartitionSpec as P

sens_scale = 0.0625
MESH = pl.DeviceIdType.MESH
VMEM_LIMIT = 60 * 1024 * 1024


def condense_kernel(tiles, inc_ref, live_ref, loads_ref, phi_ref, out_ref, acc_ref):
    step = pl.program_id(0)
    width = phi_ref.shape[1]

    @pl.when(step == 0)
    def _():
        acc_ref[...] = jnp.zeros_like(acc_ref)

    for j in range(tiles):
        t = step * tiles + j
        term = jnp.dot(
            loads_ref[:, j * width : (j + 1) * width],
            phi_ref[j],
            preferred_element_type=jnp.float32,
        )
        term = jnp.where(t < live_ref[0], term, jnp.zeros_like(term))
        b = inc_ref[t]
        acc_ref[b] = acc_ref[b] + term

    @pl.when(step == pl.num_programs(0) - 1)
    def _():
        out_ref[...] = acc_ref[...].astype(out_ref.dtype)


def recover_kernel(
    tiles, inc_ref, live_ref, loads_ref, state_ref, diag_ref, phi_ref, amp_ref, first_ref, last_ref,
    adj_ref, sens_ref, acc_ref,
):
    step = pl.program_id(0)
    width = phi_ref.shape[1]

    @pl.when(step == 0)
    def _():
        acc_ref[...] = jnp.zeros_like(acc_ref)

    total = acc_ref[...]
    for j in range(tiles):
        t = step * tiles + j
        cols = slice(j * width, (j + 1) * width)
        coupling = lax.dot_general(
            amp_ref[inc_ref[t]], phi_ref[j], (((1,), (1,)), ((), ())),
            preferred_element_type=jnp.float32,
        )
        response = diag_ref[:, cols] * loads_ref[:, cols].astype(jnp.float32) + coupling
        response = jnp.where(t < live_ref[0], response, jnp.zeros_like(response))
        adj_ref[:, cols] = response.astype(adj_ref.dtype)
        row_total = jnp.sum(response * state_ref[:, cols].astype(jnp.float32), axis=1, keepdims=True)
        member = ((first_ref[...] <= t) & (t < last_ref[...])).astype(jnp.float32)
        total = total + row_total * member
    acc_ref[...] = total

    @pl.when(step == pl.num_programs(0) - 1)
    def _():
        sens_ref[...] = acc_ref[...] * sens_scale


def flips_of(index, size):
    bits = [1 << k for k in range(size.bit_length() - 1)]
    raw = [b * (1 - 2 * ((index // b) % 2)) for b in bits]
    low = index % 2
    rest = raw[1:]
    mixed = [rest[k] + low * (rest[-1 - k] - rest[k]) for k in range(len(rest))]
    return raw, raw[:1] + mixed


def combos(count):
    return list(itertools.product((1, 0), repeat=count))


def slot_of(bits, k, c):
    before = sum(1 << (bits - 1 - j) for j in range(k))
    return before + combos(bits - 1 - k).index(c)


def exchange_kernel(wide, narrow, groups, part_ref, factor_ref, out_ref, *scratch):
    (fac, stage, stage_sem, rs_buf, rs_send, rs_recv, chunk, ag_send, ag_recv,
     amp_part, amp_buf, am_send, am_recv, ow_send, ow_recv, work) = scratch[:16]
    per_group = [scratch[16 + 9 * g : 25 + 9 * g] for g in range(len(groups))]
    own_w, own_n = lax.axis_index("wide"), lax.axis_index("narrow")
    _, flips = flips_of(own_w, wide)
    bits = len(flips)
    narrow_raw, _ = flips_of(own_n, narrow)
    peers = [own_n + sum(narrow_raw[b] for b in range(len(narrow_raw)) if i >> b & 1) for i in range(narrow)]
    partners = [own_w + f for f in flips]
    slots, stage_rows, _ = stage.shape
    stages = factor_ref.shape[0] // stage_rows
    load_rows = part_ref.shape[2]
    width = part_ref.shape[3]

    def load(s):
        return pltpu.make_async_copy(
            factor_ref.at[pl.ds(s * stage_rows, stage_rows)], stage.at[s % slots], stage_sem.at[s % slots]
        )

    for s in range(min(slots, stages)):
        load(s).start()

    barrier = pltpu.get_barrier_semaphore()
    for p in partners:
        pl.semaphore_signal(barrier, inc=1, device_id=(p, own_n), device_id_type=MESH)
    for i in range(1, narrow):
        pl.semaphore_signal(barrier, inc=1, device_id=(own_w, peers[i]), device_id_type=MESH)
    pl.semaphore_wait(barrier, bits + narrow - 1)

    sends = []

    def send(src, dst, ssem, rsem, device):
        copy = pltpu.make_async_remote_copy(
            src_ref=src, dst_ref=dst, send_sem=ssem, recv_sem=rsem, device_id=device, device_id_type=MESH
        )
        copy.start()
        sends.append(copy)
        return copy

    def place(k, c):
        return own_w + sum(flips[k + 1 + j] for j in range(len(c)) if c[j])

    def scatter_send(src, buf, ssem, rsem, k, c):
        slot = slot_of(bits, k, c)
        there = slot_of(bits, k, c[::-1]) if k == 0 else slot
        return send(
            src[min(k, 1)].at[place(k, c) + flips[k]], buf.at[there], ssem.at[slot], rsem.at[there],
            (partners[k], own_n),
        )

    def scatter_wait(buf, ssem, rsem, k, slot):
        pltpu.make_async_remote_copy(
            src_ref=buf.at[slot], dst_ref=buf.at[slot], send_sem=ssem.at[slot], recv_sem=rsem.at[slot],
            device_id=(partners[k], own_n), device_id_type=MESH,
        ).wait_recv()

    def scatter_start(src, buf, ssem, rsem):
        return {c: scatter_send(src, buf, ssem, rsem, 0, c) for c in combos(bits - 1)}

    def scatter_step(src, buf, ssem, rsem, pending, k, finish):
        following = {}
        for c in combos(bits - 1 - k):
            slot = slot_of(bits, k, c)
            scatter_wait(buf, ssem, rsem, k, slot)
            d = place(k, c)
            held = src[min(k, 1)]
            total = (held[d].astype(jnp.float32) + buf[slot].astype(jnp.float32)).astype(held.dtype)
            if k == bits - 1:
                finish(total)
            else:
                src[1][d] = total
                if c[0]:
                    following[c[1:]] = scatter_send(src, buf, ssem, rsem, k + 1, c[1:])
        return following

    def gather_send(buf, ssem, rsem, k):
        pending = []
        for c in combos(bits - 1 - k):
            slot = slot_of(bits, k, c)
            d = place(k, c)
            pending.append(send(buf.at[d], buf.at[d], ssem.at[slot], rsem.at[slot], (partners[k], own_n)))
        return pending

    def convert(lo, hi):
        for s in range(lo, hi):
            load(s).wait()
            rows = stage_rows // 8

            def some(r, carry, s=s):
                here = pl.multiple_of(r * rows, rows)
                fac[pl.ds(s * stage_rows + here, rows), :] = stage[s % slots, pl.ds(here, rows), :].astype(fac.dtype)
                return carry

            lax.fori_loop(0, 8, some, 0)
            if s + slots < stages:
                load(s + slots).start()

    def keep_chunk(total):
        chunk[0] = total

    pending = scatter_start((part_ref, work), rs_buf, rs_send, rs_recv)
    for k in range(bits):
        convert(stages * k // (bits + 1), stages * (k + 1) // (bits + 1))
        pending = scatter_step((part_ref, work), rs_buf, rs_send, rs_recv, pending, k, keep_chunk)
    order = [i for group in groups for i in group]
    chunk_copies = {
        i: send(chunk.at[0], chunk.at[i], ag_send.at[i - 1], ag_recv.at[i - 1], (own_w, peers[i]))
        for i in order if i
    }
    convert(stages * bits // (bits + 1), stages)

    state = [None] * len(groups)
    amp_copies = []

    def run(g, stage_index):
        lhs, lhs2, part, p_buf, p_send, p_recv, image, i_send, i_recv = per_group[g]
        group = groups[g]
        if stage_index == 0:
            for a, i in enumerate(group):
                if i:
                    chunk_copies[i].wait_recv()
                for b in range(chunk.shape[1]):
                    lhs[a * load_rows : (a + 1) * load_rows, b * width : (b + 1) * width] = chunk[i, b]
            cols = part.shape[2]

            def one(d, carry):
                here = pl.multiple_of(d * cols, cols)
                part[d] = jnp.dot(
                    lhs[...], fac[:, pl.ds(here, cols)], preferred_element_type=jnp.float32
                ).astype(part.dtype)
                return carry

            lax.fori_loop(0, wide, one, 0)
            state[g] = scatter_start((part, part), p_buf, p_send, p_recv)
        elif stage_index <= bits:
            def keep(total):
                image[own_w] = total

            state[g] = scatter_step((part, part), p_buf, p_send, p_recv, state[g], stage_index - 1, keep)
            if stage_index == bits:
                state[g] = gather_send(image, i_send, i_recv, bits - 1)
        else:
            k = 2 * bits - stage_index
            for copy in state[g]:
                copy.wait_recv()
            if k > 0:
                state[g] = gather_send(image, i_send, i_recv, k - 1)
                return
            cols = image.shape[2]
            for d in range(wide):
                lhs2[:, d * cols : (d + 1) * cols] = image[d]
            rows = 2 * width

            def two(r, carry):
                here = pl.multiple_of(r * rows, rows)
                value = lax.dot_general(
                    lhs2[...], fac[pl.ds(here, rows), :], (((1,), (1,)), ((), ())),
                    preferred_element_type=jnp.float32,
                ).astype(amp_part.dtype)
                for a, i in enumerate(group):
                    for h in range(2):
                        amp_part[i, 2 * r + h] = value[
                            a * load_rows : (a + 1) * load_rows, h * width : (h + 1) * width
                        ]
                return carry

            lax.fori_loop(0, fac.shape[0] // rows, two, 0)
            for i in group:
                if i:
                    amp_copies.append((i, send(
                        amp_part.at[i], amp_buf.at[i - 1], am_send.at[i - 1], am_recv.at[i - 1],
                        (own_w, peers[i]),
                    )))

    last = 2 * bits
    for tick in range(last + len(groups)):
        for g in range(len(groups)):
            if 0 <= tick - g <= last:
                run(g, tick - g)

    total = amp_part[0].astype(jnp.float32)
    for i, copy in amp_copies:
        copy.wait_recv()
        total = total + amp_buf[i - 1].astype(jnp.float32)
    out_ref[own_w] = total.astype(out_ref.dtype)
    for k in range(bits - 1, -1, -1):
        for copy in gather_send(out_ref, ow_send, ow_recv, k):
            copy.wait_recv()
    for copy in sends:
        copy.wait_send()


def exchange(partial, factor, wide, narrow, groups):
    _, blocks, load_rows, width = partial.shape
    own_rows, own_cols = factor.shape
    cols = own_cols // wide
    bf = partial.dtype
    dma = pltpu.SemaphoreType.DMA
    stage_rows = min(128, own_rows)
    scratch = [
        pltpu.VMEM((own_rows, own_cols), bf),
        pltpu.VMEM((4, stage_rows, own_cols), factor.dtype),
        dma((4,)),
        pltpu.VMEM((wide - 1, blocks, load_rows, width), bf), dma((wide - 1,)), dma((wide - 1,)),
        pltpu.VMEM((narrow, blocks, load_rows, width), bf), dma((narrow - 1,)), dma((narrow - 1,)),
        pltpu.VMEM((narrow, blocks, load_rows, width), bf),
        pltpu.VMEM((narrow - 1, blocks, load_rows, width), bf), dma((narrow - 1,)), dma((narrow - 1,)),
        dma((wide - 1,)), dma((wide - 1,)),
        pltpu.VMEM(partial.shape, bf),
    ]
    for group in groups:
        rows = len(group) * load_rows
        scratch += [
            pltpu.VMEM((rows, own_rows), bf), pltpu.VMEM((rows, own_cols), bf),
            pltpu.VMEM((wide, rows, cols), bf),
            pltpu.VMEM((wide - 1, rows, cols), bf), dma((wide - 1,)), dma((wide - 1,)),
            pltpu.VMEM((wide, rows, cols), bf), dma((wide - 1,)), dma((wide - 1,)),
        ]
    return pl.pallas_call(
        functools.partial(exchange_kernel, wide, narrow, groups),
        out_shape=jax.ShapeDtypeStruct(partial.shape, bf),
        in_specs=[pl.BlockSpec(memory_space=pltpu.VMEM), pl.BlockSpec(memory_space=pl.ANY)],
        out_specs=pl.BlockSpec(memory_space=pltpu.VMEM),
        scratch_shapes=scratch,
        compiler_params=pltpu.CompilerParams(
            collective_id=0, has_side_effects=True, vmem_limit_bytes=VMEM_LIMIT
        ),
        name="exchange",
    )(partial, factor)


def groups_of(narrow):
    order = [0] + list(range(narrow - 1, 0, -1))
    size = max(1, narrow // 2)
    return [order[k : k + size] for k in range(0, narrow, size)]


def body(loads, state, modal_diag, phi, incidence, sizes, factor):
    load_cols = loads.shape[0]
    tile_count, width, _ = phi.shape
    subs_local = sizes.shape[0]
    wide, narrow = lax.axis_size("wide"), lax.axis_size("narrow")
    own_blocks = factor.shape[0] // width
    block_count = own_blocks * wide
    running = jnp.cumsum(sizes)
    live = running[-1:]
    tiles = min(16, tile_count)
    steps = tile_count // tiles
    params = pltpu.CompilerParams(dimension_semantics=("arbitrary",), vmem_limit_bytes=VMEM_LIMIT)
    row_spec = pl.BlockSpec((load_cols, tiles * width), lambda s, *_: (0, s))
    phi_spec = pl.BlockSpec((tiles, width, width), lambda s, *_: (s, 0, 0))
    amp_spec = pl.BlockSpec((block_count, load_cols, width), lambda s, *_: (0, 0, 0))
    sub_spec = pl.BlockSpec((1, subs_local), lambda s, *_: (0, 0))
    sens_spec = pl.BlockSpec((load_cols, subs_local), lambda s, *_: (0, 0))

    partial = pl.pallas_call(
        functools.partial(condense_kernel, tiles),
        out_shape=jax.ShapeDtypeStruct((block_count, load_cols, width), jnp.bfloat16),
        grid_spec=pltpu.PrefetchScalarGridSpec(
            num_scalar_prefetch=2, grid=(steps,), in_specs=[row_spec, phi_spec], out_specs=amp_spec,
            scratch_shapes=[pltpu.VMEM((block_count, load_cols, width), jnp.float32)],
        ),
        compiler_params=params,
        name="condense",
    )(incidence, live, loads, phi)
    amp = exchange(
        partial.reshape(wide, own_blocks, load_cols, width), factor, wide, narrow, groups_of(narrow)
    ).reshape(block_count, load_cols, width)
    adjoint, sensitivity = pl.pallas_call(
        functools.partial(recover_kernel, tiles),
        out_shape=(
            jax.ShapeDtypeStruct(loads.shape, jnp.bfloat16),
            jax.ShapeDtypeStruct((load_cols, subs_local), jnp.float32),
        ),
        grid_spec=pltpu.PrefetchScalarGridSpec(
            num_scalar_prefetch=2, grid=(steps,),
            in_specs=[
                row_spec, row_spec, pl.BlockSpec((1, tiles * width), lambda s, *_: (0, s)),
                phi_spec, amp_spec, sub_spec, sub_spec,
            ],
            out_specs=(row_spec, sens_spec),
            scratch_shapes=[pltpu.VMEM((load_cols, subs_local), jnp.float32)],
        ),
        compiler_params=params,
        name="recover",
    )(
        incidence, live, loads, state, modal_diag.reshape(1, -1), phi, amp,
        (running - sizes).reshape(1, -1), running.reshape(1, -1),
    )
    return (adjoint, sensitivity)


def solution(mesh):
    return jax.shard_map(
        body,
        mesh=mesh,
        in_specs=(
            P("narrow", "wide"),
            P("narrow", "wide"),
            P("wide"),
            P("wide", None, None),
            P("wide"),
            P("wide"),
            P("wide", "narrow"),
        ),
        out_specs=(P("narrow", "wide"), P("narrow", "wide")),
        check_vma=False,
    )
```

time: 345 us -> 151 us (0.44)
  waiting for transfers between devices: 216 us -> 0 us
  Pallas kernels: 0 us -> 147 us
  matrix products: 91.9 us -> 0 us
  local copies, waits for them, and re-layouts: 21.5 us -> 1.29 us
  between operations: 13.9 us -> 0.65 us
    pallas_call x0 -> x3, Pallas kernels: none -> 147 us  [the longest x1 113 us: exchange(): pl.pallas_call(functools.partial(exchange_kernel, wide, narrow, groups),...]
    dot_general x6 -> x0, matrix products: 91.9 us -> none  [the longest x1 33.8 us: body(): jnp.dot(lax.all_gather(own_loads, 'narrow', axis=0, tiled=True), factor,...]
    reduce_scatter x2 -> x0, waiting for transfers between devices: 80.4 us -> none  [the longest x1 53.9 us: body(): lax.psum_scatter(partial_value, 'wide', scatter_dimension=1, tiled=True)]
    all_gather x2 -> x0, waiting for transfers between devices: 74.9 us -> none  [the longest x1 47.2 us: body(): lax.all_gather(own_loads, 'narrow', axis=0, tiled=True)]
    psum x1 -> x0, waiting for transfers between devices: 60.7 us -> none  [body(): image = lax.psum(image.astype(jnp.bfloat16), 'wide').astype(jnp.float32)]
    unnamed x5 -> x2, local copies, waits for them, and re-layouts: 6.59 us -> 0.01 us
    transpose x1 -> x0, local copies, waits for them, and re-layouts: 5.59 us -> none  [body(): jnp.einsum('tn,ltm->lnm', chooser, tile_terms, precision=lax.Precision.HI...]
    reshape x3 -> x1, local copies, waits for them, and re-layouts: 5.72 us -> 0.76 us  [the longest x1 2.78 us: body(): response.astype(jnp.bfloat16).reshape(load_cols, tile_count * block_rows)]
  transfers between devices with their start and end apart: 5 -> 0, of which waited for: 5 -> 0; matrix products, arithmetic and copies ran while one was open for 0% -> 0% of each run, Pallas kernels for 0% -> 0%
where the time goes in v1:
time: 151 us; the launch traced here: 150 us
  Pallas kernels  147 us (97%)
    pallas_call x1, Pallas kernels, exchange(): pl.pallas_call(functools.partial(exchange_kernel, wide, narrow, groups),...  113 us
    pallas_call x1, Pallas kernels, body(): pl.pallas_call(functools.partial(recover_kernel, tiles), out_shape=(jax.S...  19 us
    pallas_call x1, Pallas kernels, body(): pl.pallas_call(functools.partial(condense_kernel, tiles), out_shape=jax.S...  15.1 us

profile of v1, /device:TPU:0, one launch (start us, length us, event | category | flops | bytes accessed | tf_op | source)
XLA Modules:
  0.0 150.3 jit_solution(2593129947633059189)
XLA Ops:
  0.6 0.8 copy.10
  1.4 0.2 reduce-window.4
  1.6 0.5 slice.8
  2.1 0.1 reduce
  2.2 0.0 copy-start
  2.2 1.2 subtract_bitcast_fusion.first_ref
  3.4 15.1 %condense.1 = bf16[128,64,128]{2,1,0:T(8,128)(2,1)} custom-call(s32[256]{0:T(256)} %inc_ref.3, s32[1]{0:T(128)} %bitcast.1.live_ref, bf16[64,32768]{1,0:T(8,128)(2,1)} %loads_ref.3, bf16[256,128,128]{2,1,0:T(8,128)(2,1)} %phi_ref.3), custom_call_target="tpu_custom_call" | custom-call | tf_op jit(solution)/shard_map/condense/pallas_call | solution.py:345
  18.5 0.0 copy-done
  18.5 112.9 %exchange.1 = bf16[8,16,64,128]{3,2,1,0:T(8,128)(2,1)} custom-call(bf16[8,16,64,128]{3,2,1,0:T(8,128)(2,1)} %bitcast.9, f32[2048,4096]{1,0:T(8,128)} %factor_ref.1), custom_call_target="tpu_custom_call" | custom-call | tf_op jit(solution)/shard_map/exchange/pallas_call | solution.py:308
  131.3 19.0 %recover.1 = (bf16[64,32768]{1,0:T(8,128)(2,1)}, f32[64,128]{1,0:T(8,128)}) custom-call(s32[256]{0:T(256)} %inc_ref.3, s32[1]{0:T(128)} %bitcast.1.live_ref, bf16[64,32768]{1,0:T(8,128)(2,1)} %loads_ref.3, bf16[64,32768]{1,0:T(8,128)(2,1)} %state_ref.1, f32[1,32768]{1,0:T(1,128)} %bitcast.10, bf16[256,128,128]{2,1,0:T(8,128)(2,1)} %phi_ref.3, ...), custom_call_target="tpu_custom_call" | custom-call | tf_op jit(solution)/shard_map/recover/pallas_call | solution.py:358
Async XLA Ops:
  2.2 16.3 %copy-start = (s32[128]{0:T(128)}, s32[128]{0:T(128)S(1)}, u32[]{:S(2)}) copy-start(s32[128]{0:T(128)S(1)} %reduce) | copy-start | bytes 1540

commit v2 on v1

--- a/solution.py
+++ b/solution.py
@@ -10,6 +10,7 @@
 sens_scale = 0.0625
 MESH = pl.DeviceIdType.MESH
 VMEM_LIMIT = 60 * 1024 * 1024
+STEP_TILES = 64
 
 
 def condense_kernel(tiles, inc_ref, live_ref, loads_ref, phi_ref, out_ref, acc_ref):
@@ -333,7 +334,7 @@
     block_count = own_blocks * wide
     running = jnp.cumsum(sizes)
     live = running[-1:]
-    tiles = min(16, tile_count)
+    tiles = min(STEP_TILES, tile_count)
     steps = tile_count // tiles
     params = pltpu.CompilerParams(dimension_semantics=("arbitrary",), vmem_limit_bytes=VMEM_LIMIT)
     row_spec = pl.BlockSpec((load_cols, tiles * width), lambda s, *_: (0, s))

time: 151 us -> 139 us (0.921)
  Pallas kernels: 147 us -> 136 us
    pallas_call x1, Pallas kernels: 15.1 us -> 9.44 us  [body(): pl.pallas_call(functools.partial(condense_kernel, tiles), out_shape=jax.S...]
    pallas_call x1, Pallas kernels: 19 us -> 13.3 us  [body(): pl.pallas_call(functools.partial(recover_kernel, tiles), out_shape=(jax.S...]
where the time goes in v2:
time: 139 us
  Pallas kernels  136 us (98%)
  other arithmetic  1.48 us (1%)
    pallas_call x1, Pallas kernels, exchange(): pl.pallas_call(functools.partial(exchange_kernel, wide, narrow, groups),...  113 us
    pallas_call x1, Pallas kernels, body(): pl.pallas_call(functools.partial(recover_kernel, tiles), out_shape=(jax.S...  13.3 us
    pallas_call x1, Pallas kernels, body(): pl.pallas_call(functools.partial(condense_kernel, tiles), out_shape=jax.S...  9.44 us

profile of v2, /device:TPU:0, one launch (start us, length us, event | category | flops | bytes accessed | tf_op | source)
XLA Modules:
  0.0 139.0 jit_solution(3483128073917661)
XLA Ops:
  0.6 0.8 copy.10
  1.4 0.2 reduce-window.4
  1.6 0.5 slice.8
  2.1 0.1 reduce
  2.2 0.0 copy-start
  2.2 1.2 subtract_bitcast_fusion.first_ref
  3.4 9.4 %condense.1 = bf16[128,64,128]{2,1,0:T(8,128)(2,1)} custom-call(s32[256]{0:T(256)} %inc_ref.3, s32[1]{0:T(128)} %bitcast.1.live_ref, bf16[64,32768]{1,0:T(8,128)(2,1)} %loads_ref.3, bf16[256,128,128]{2,1,0:T(8,128)(2,1)} %phi_ref.3), custom_call_target="tpu_custom_call" | custom-call | tf_op jit(solution)/shard_map/condense/pallas_call | solution.py:346
  12.8 0.0 copy-done
  12.8 112.8 %exchange.1 = bf16[8,16,64,128]{3,2,1,0:T(8,128)(2,1)} custom-call(bf16[8,16,64,128]{3,2,1,0:T(8,128)(2,1)} %bitcast.9, f32[2048,4096]{1,0:T(8,128)} %factor_ref.1), custom_call_target="tpu_custom_call" | custom-call | tf_op jit(solution)/shard_map/exchange/pallas_call | solution.py:309
  125.7 13.3 %recover.1 = (bf16[64,32768]{1,0:T(8,128)(2,1)}, f32[64,128]{1,0:T(8,128)}) custom-call(s32[256]{0:T(256)} %inc_ref.3, s32[1]{0:T(128)} %bitcast.1.live_ref, bf16[64,32768]{1,0:T(8,128)(2,1)} %loads_ref.3, bf16[64,32768]{1,0:T(8,128)(2,1)} %state_ref.1, f32[1,32768]{1,0:T(1,128)} %bitcast.10, bf16[256,128,128]{2,1,0:T(8,128)(2,1)} %phi_ref.3, ...), custom_call_target="tpu_custom_call" | custom-call | tf_op jit(solution)/shard_map/recover/pallas_call | solution.py:359
Async XLA Ops:
  2.2 10.7 %copy-start = (s32[128]{0:T(128)}, s32[128]{0:T(128)S(1)}, u32[]{:S(2)}) copy-start(s32[128]{0:T(128)S(1)} %reduce) | copy-start | bytes 1540
